TPU v7x, 128 devices: a whole 4x4x4 slice. The times are simulated.
128 devices in a mesh: edata: 8 (over y, x_hi), tensor: 16 (over z, x_lo, core).
Axes of the slice: x: 4 (x_hi: 2, x_lo: 2; x = x_hi * 2 + x_lo), y: 4, z: 4, core: 2. Of those that a mesh axis runs over, the one named last changes fastest.
Arguments:
- tokens: bfloat16 [2048, 6144], P('tensor', 'edata'), may hold values from -6 to 6
- expert_ids: int32 [2048, 2], P('tensor'), may hold values from 0 to 7, as said below
- route_weight: float32 [2048, 2], P('tensor'), may hold values from 0.25 to 1
- up_weight: bfloat16 [2, 6144, 16384], P(None, 'edata', 'tensor'), may hold values from -0.078125 to 0.078125
- down_weight: bfloat16 [2, 16384, 6144], P(None, 'tensor', 'edata'), may hold values from -0.046875 to 0.046875
- target_up: bfloat16 [2, 6144, 16384], P(None, 'edata', 'tensor'), may hold values from -0.078125 to 0.078125
- target_down: bfloat16 [2, 16384, 6144], P(None, 'tensor', 'edata'), may hold values from -0.046875 to 0.046875
- cotangent: bfloat16 [2048, 6144], P('tensor', 'edata'), may hold values from -6 to 6
Outputs:
- mixed: bfloat16 [2048, 6144], P('tensor', 'edata')
- grad_tokens: bfloat16 [2048, 6144], P('tensor', 'edata')
- grad_up: bfloat16 [2, 6144, 16384], P(None, 'edata', 'tensor')
- grad_down: bfloat16 [2, 16384, 6144], P(None, 'tensor', 'edata')
- target_mixed: bfloat16 [2048, 6144], P('tensor', 'edata')
Inputs may be any that keep to these rules, and one draw needn't show every extreme that they name: `expert_ids`: every token names 2 different experts. Among the 128 tokens of one tensor index no expert is named by more than 48 tokens, and expert 0 is named by exactly 48.
All inputs are finite; a program needn't handle non-finite values.
Results may differ from a plain program's by a relative error of at most 0.03.
Values may be sent and summed in bfloat16 or wider, within the bound.
No kernel may reach another device: no remote copies, remote signals or barrier semaphores. Data moves between devices by JAX's collectives and lax.ppermute only.
A program may use at most 128 MiB of HBM per device.

v0:
```python
import jax
import jax.numpy as jnp
from jax import lax
from jax.sharding import PartitionSpec as P

EXP_WIN = 2
CAP = 48


def tables(expert_ids, route_weight):
    placed_list, portion_list = ([], [])
    for expert in range(EXP_WIN):
        chosen = expert_ids == expert
        listed = jnp.any(chosen, axis=1)
        position = jnp.cumsum(listed.astype(jnp.int32)) - 1
        placed = (position[None, :] == jnp.arange(CAP, dtype=jnp.int32)[:, None]) & listed[None, :]
        weight = jnp.sum(jnp.where(chosen, route_weight, 0.0), axis=1)
        placed_list.append(placed)
        portion_list.append(jnp.where(placed, weight[None, :], 0.0))
    onehot = jnp.stack(placed_list, axis=1).astype(jnp.bfloat16)
    combine = jnp.stack(portion_list, axis=1)
    return (onehot, combine)


def combined(owner_out, combine):
    return jnp.einsum("ced,cet->td", owner_out, combine, precision=lax.Precision.HIGHEST).astype(
        jnp.bfloat16
    )


def silu_round(summed):
    return jax.nn.silu(summed).astype(jnp.bfloat16)


def shards(
    tokens, expert_ids, route_weight, up_weight, down_weight, target_up, target_down, cotangent
):
    onehot, combine = tables(expert_ids, route_weight)
    picked = jnp.einsum("cet,td->ced", onehot, tokens, preferred_element_type=jnp.float32).astype(
        jnp.bfloat16
    )
    scaled = jnp.einsum(
        "cet,td->ced", combine, cotangent.astype(jnp.float32), precision=lax.Precision.HIGHEST
    ).astype(jnp.bfloat16)
    gathered_x, gathered_g = (
        lax.all_gather(picked, "tensor", axis=0, tiled=True),
        lax.all_gather(scaled, "tensor", axis=0, tiled=True),
    )
    routed = gathered_x.shape[0]
    share_rows = routed // lax.axis_size("edata")
    owner_rows = routed // lax.axis_size("tensor")

    def edata_sum(term_fn, act_fn):
        summed = lax.psum_scatter(
            term_fn(jnp.int32(0), share_rows * lax.axis_size("edata")).astype(jnp.bfloat16),
            "edata",
            scatter_dimension=0,
            tiled=True,
        ).astype(jnp.float32)
        acted = lax.all_gather(act_fn(summed), "edata", axis=0, tiled=True)
        return (acted, summed)

    def tensor_sum(term_fn):
        return lax.psum_scatter(
            term_fn(jnp.int32(0), owner_rows * lax.axis_size("tensor")).astype(jnp.bfloat16),
            "tensor",
            scatter_dimension=0,
            tiled=True,
        ).astype(jnp.float32)

    def up_term(source, weight):

        def partial_up(begin_row, row_count):
            return jnp.einsum("red,edf->ref", source, weight, preferred_element_type=jnp.float32)

        return partial_up

    def down_term(source, weight):

        def partial_down(begin_row, row_count):
            return jnp.einsum("ref,efd->red", source, weight, preferred_element_type=jnp.float32)

        return partial_down

    def back_term(begin_row, row_count):
        return jnp.einsum(
            "red,efd->ref", gathered_g, down_weight, preferred_element_type=jnp.float32
        )

    blend_up = (0.75 * target_up.astype(jnp.float32) + 0.25 * up_weight.astype(jnp.float32)).astype(
        jnp.bfloat16
    )
    blend_down = (
        0.75 * target_down.astype(jnp.float32) + 0.25 * down_weight.astype(jnp.float32)
    ).astype(jnp.bfloat16)
    active, hidden_pre = edata_sum(up_term(gathered_x, up_weight), silu_round)
    owner_out = tensor_sum(down_term(active, down_weight))
    mixed = combined(owner_out, combine)
    grad_down = jnp.einsum(
        "ref,red->efd", active, gathered_g, preferred_element_type=jnp.float32
    ).astype(jnp.bfloat16)

    def grad_act(summed):
        logistic = jax.nn.sigmoid(hidden_pre)
        return (summed * logistic * (1.0 + hidden_pre * (1.0 - logistic))).astype(jnp.bfloat16)

    grad_pre, unused = edata_sum(back_term, grad_act)
    grad_up = jnp.einsum(
        "red,ref->edf", gathered_x, grad_pre, preferred_element_type=jnp.float32
    ).astype(jnp.bfloat16)

    def grad_term(begin_row, row_count):
        return jnp.einsum("ref,edf->red", grad_pre, up_weight, preferred_element_type=jnp.float32)

    grad_rows = tensor_sum(grad_term)
    grad_tokens = combined(grad_rows, combine)
    target_active, unused_pre = edata_sum(up_term(gathered_x, blend_up), silu_round)
    target_out = tensor_sum(down_term(target_active, blend_down))
    target_mixed = combined(target_out, combine)
    return (mixed, grad_tokens, grad_up, grad_down, target_mixed)


def solution(mesh):
    return jax.shard_map(
        shards,
        mesh=mesh,
        in_specs=(
            P("tensor", "edata"),
            P("tensor", None),
            P("tensor", None),
            P(None, "edata", "tensor"),
            P(None, "tensor", "edata"),
            P(None, "edata", "tensor"),
            P(None, "tensor", "edata"),
            P("tensor", "edata"),
        ),
        out_specs=(
            P("tensor", "edata"),
            P("tensor", "edata"),
            P(None, "edata", "tensor"),
            P(None, "tensor", "edata"),
            P("tensor", "edata"),
        ),
        check_vma=False,
    )
```

profile of v0, /device:TPU:4, one launch (start us, length us, event | category | flops | bytes accessed | tf_op | source)
XLA Modules:
  0.0 728.4 jit_solution(15373005583422794436)
XLA Ops:
  7.2 0.7 fusion.27
  8.5 0.2 reduce-window.16
  8.8 0.8 convolution_convert_fusion.3
  9.7 0.7 select_reduce_fusion.1
  10.5 1.9 convolution_convert_fusion.2
  12.4 34.4 %all-gather.6.cloned.1.call-done = bf16[768,2,768]{2,0,1:T(8,128)(2,1)} async-done(((bf16[48,2,768]{2,0,1:T(8,128)(2,1)}), bf16[768,2,768]{2,0,1:T(8,128)(2,1)}) %all-gather.6.cloned.1.call-update) | async-done | bytes 2359312 | tf_op jit(solution)/shard_map/all_gather | solution.py:46
  46.8 7.9 %convert_bitcast_fusion = bf16[768,2,1024]{2,0,1:T(8,128)(2,1)} fusion(bf16[768,2,768]{2,0,1:T(8,128)(2,1)} %all-gather.6.cloned.1.call-done, bf16[2,768,1024]{2,1,0:T(8,128)(2,1)} %param.11, bf16[2,768,1024]{2,1,0:T(8,128)(2,1)} %param.13), kind=kOutput, calls=%fused_computation.4 | convolution fusion | flops 2426929152 | bytes 11796480 | tf_op jit(solution)/shard_map/red,edf->ref/dot_general | solution.py:74
  54.8 28.7 %all-gather.10.cloned.1.call-done = bf16[768,2,768]{2,0,1:T(8,128)(2,1)} async-done(((bf16[48,2,768]{2,0,1:T(8,128)(2,1)}), bf16[768,2,768]{2,0,1:T(8,128)(2,1)}) %all-gather.10.cloned.1.call-update) | async-done | bytes 2359312 | tf_op jit(solution)/shard_map/all_gather | solution.py:47
  83.5 5.7 convert_bitcast_fusion.1
  89.2 1.8 copy-done.3
  91.1 5.6 convert_bitcast_fusion.2
  96.7 67.7 %reduce-scatter.15.cloned.1.call-done = bf16[96,2,1024]{2,0,1:T(8,128)(2,1)} async-done(((bf16[768,2,1024]{2,0,1:T(8,128)(2,1)}), bf16[96,2,1024]{2,0,1:T(8,128)(2,1)}) %reduce-scatter.15.cloned.1.call-update) | async-done | bytes 393232 | tf_op jit(solution)/shard_map/reduce_scatter | solution.py:54
  164.4 2.0 fusion.12
  166.5 80.2 %reduce-scatter.11.cloned.1.call-done = bf16[96,2,1024]{2,0,1:T(8,128)(2,1)} async-done(((bf16[768,2,1024]{2,0,1:T(8,128)(2,1)}), bf16[96,2,1024]{2,0,1:T(8,128)(2,1)}) %reduce-scatter.11.cloned.1.call-update) | async-done | bytes 393232 | tf_op jit(solution)/shard_map/reduce_scatter | solution.py:54
  246.7 82.3 %reduce-scatter.7.cloned.1.call-done = bf16[96,2,1024]{2,0,1:T(8,128)(2,1)} async-done(((bf16[768,2,1024]{2,0,1:T(8,128)(2,1)}), bf16[96,2,1024]{2,0,1:T(8,128)(2,1)}) %reduce-scatter.7.cloned.1.call-update) | async-done | bytes 393232 | tf_op jit(solution)/shard_map/reduce_scatter | solution.py:54
  329.0 2.4 fusion.19
  331.5 0.7 all-gather.12.cloned.1.call-update
  332.2 60.3 %all-gather.14.cloned.1.call-done = bf16[768,2,1024]{2,0,1:T(8,128)(2,1)} async-done(((bf16[96,2,1024]{2,0,1:T(8,128)(2,1)}), bf16[768,2,1024]{2,0,1:T(8,128)(2,1)}) %all-gather.14.cloned.1.call-update) | async-done | bytes 3145744 | tf_op jit(solution)/shard_map/all_gather | solution.py:60
  392.5 7.0 convert_bitcast_fusion.3
  399.6 56.3 %all-gather.8.cloned.1.call-done = bf16[768,2,1024]{2,0,1:T(8,128)(2,1)} async-done(((bf16[96,2,1024]{2,0,1:T(8,128)(2,1)}), bf16[768,2,1024]{2,0,1:T(8,128)(2,1)}) %all-gather.8.cloned.1.call-update) | async-done | bytes 3145744 | tf_op jit(solution)/shard_map/all_gather | solution.py:60
  455.9 6.8 convert_bitcast_fusion.5
  462.8 0.2 reduce-scatter.13.cloned.1.call-start
  463.0 56.3 %all-gather.12.cloned.1.call-done = bf16[768,2,1024]{2,0,1:T(8,128)(2,1)} async-done(((bf16[96,2,1024]{2,0,1:T(8,128)(2,1)}), bf16[768,2,1024]{2,0,1:T(8,128)(2,1)}) %all-gather.12.cloned.1.call-update) | async-done | bytes 3145744 | tf_op jit(solution)/shard_map/all_gather | solution.py:60
  519.3 5.9 convert_bitcast_fusion.4
  525.3 7.1 convolution_convert_fusion
  532.4 4.1 convolution_convert_fusion.1
  536.4 50.9 %reduce-scatter.17.cloned.1.call-done = bf16[48,2,768]{2,0,1:T(8,128)(2,1)} async-done(((bf16[768,2,768]{2,0,1:T(8,128)(2,1)}), bf16[48,2,768]{2,0,1:T(8,128)(2,1)}) %reduce-scatter.17.cloned.1.call-update) | async-done | bytes 147472 | tf_op jit(solution)/shard_map/reduce_scatter | solution.py:64
  587.3 2.0 fusion.8
  589.3 64.3 %reduce-scatter.9.cloned.1.call-done = bf16[48,2,768]{2,0,1:T(8,128)(2,1)} async-done(((bf16[768,2,768]{2,0,1:T(8,128)(2,1)}), bf16[48,2,768]{2,0,1:T(8,128)(2,1)}) %reduce-scatter.9.cloned.1.call-update) | async-done | bytes 147472 | tf_op jit(solution)/shard_map/reduce_scatter | solution.py:64
  653.6 2.0 fusion.6
  655.5 64.4 %reduce-scatter.13.cloned.1.call-done = bf16[48,2,768]{2,0,1:T(8,128)(2,1)} async-done(((bf16[768,2,768]{2,0,1:T(8,128)(2,1)}), bf16[48,2,768]{2,0,1:T(8,128)(2,1)}) %reduce-scatter.13.cloned.1.call-update) | async-done | bytes 147472 | tf_op jit(solution)/shard_map/reduce_scatter | solution.py:64
  719.9 2.0 fusion.7
  (42 shorter events, 1.3 us)
Async XLA Ops:
  7.2 1.6 copy-start
  7.2 39.6 %all-gather.6.cloned.1.call-start = ((), (), s32[]{:S(2)}) async-start(), calls=%async_computation.6 | async-start | bytes 2506752 | tf_op jit(solution)/shard_map/all_gather | solution.py:46
  9.7 73.8 %all-gather.10.cloned.1.call-start = ((), (), s32[]{:S(2)}) async-start(), calls=%async_computation.10 | async-start | bytes 2506752 | tf_op jit(solution)/shard_map/all_gather | solution.py:47
  12.4 152.1 %reduce-scatter.15.cloned.1.call-start = ((), (), s32[]{:S(2)}) async-start(), calls=%async_computation.14 | async-start | bytes 3538944 | tf_op jit(solution)/shard_map/reduce_scatter | solution.py:54
  54.7 28.8 %copy-start.2 = (bf16[2,1024,768]{2,1,0:T(8,128)(2,1)S(1)}, bf16[2,1024,768]{2,1,0:T(8,128)(2,1)}, u32[]{:S(2)}) copy-start(bf16[2,1024,768]{2,1,0:T(8,128)(2,1)} %param.12) | copy-start | bytes 9437188
  54.7 192.0 %reduce-scatter.11.cloned.1.call-start = ((), (), s32[]{:S(2)}) async-start(), calls=%async_computation.11 | async-start | bytes 3538944 | tf_op jit(solution)/shard_map/reduce_scatter | solution.py:54
  89.2 1.9 copy-start.3
  89.2 239.8 %reduce-scatter.7.cloned.1.call-start = ((), (), s32[]{:S(2)}) async-start(), calls=%async_computation.7 | async-start | bytes 3538944 | tf_op jit(solution)/shard_map/reduce_scatter | solution.py:54
  96.7 295.8 %copy-start.1 = (bf16[2,1024,768]{2,1,0:T(8,128)(2,1)S(1)}, bf16[2,1024,768]{2,1,0:T(8,128)(2,1)}, u32[]{:S(2)}) copy-start(bf16[2,1024,768]{2,1,0:T(8,128)(2,1)} %param.14) | copy-start | bytes 9437188
  96.7 295.8 %all-gather.14.cloned.1.call-start = ((), (), s32[]{:S(2)}) async-start(), calls=%async_computation.15 | async-start | bytes 3538944 | tf_op jit(solution)/shard_map/all_gather | solution.py:60
  166.4 289.5 %all-gather.8.cloned.1.call-start = ((), (), s32[]{:S(2)}) async-start(), calls=%async_computation.8 | async-start | bytes 3538944 | tf_op jit(solution)/shard_map/all_gather | solution.py:60
  331.4 187.9 %all-gather.12.cloned.1.call-start = ((), (), s32[]{:S(2)}) async-start(), calls=%async_computation.12 | async-start | bytes 3538944 | tf_op jit(solution)/shard_map/all_gather | solution.py:60
  332.2 255.1 %reduce-scatter.17.cloned.1.call-start = ((), (), s32[]{:S(2)}) async-start(), calls=%async_computation.16 | async-start | bytes 2506752 | tf_op jit(solution)/shard_map/reduce_scatter | solution.py:64
  399.5 119.7 %copy-start.4 = (bf16[2,768,1024]{2,1,0:T(8,128)(2,1)S(1)}, bf16[2,768,1024]{2,1,0:T(8,128)(2,1)}, u32[]{:S(2)}) copy-start(bf16[2,768,1024]{2,1,0:T(8,128)(2,1)} %param.11) | copy-start | bytes 9437188
  399.6 254.0 %reduce-scatter.9.cloned.1.call-start = ((), (), s32[]{:S(2)}) async-start(), calls=%async_computation.9 | async-start | bytes 2506752 | tf_op jit(solution)/shard_map/reduce_scatter | solution.py:64
  462.8 257.2 %reduce-scatter.13.cloned.1.call-start = ((), (), s32[]{:S(2)}) async-start(), calls=%async_computation.13 | async-start | bytes 2506752 | tf_op jit(solution)/shard_map/reduce_scatter | solution.py:64
  525.2 7.1 copy-start.5
  525.2 7.1 copy-start.6
Sparse Core Ops, SparseCore 0:
  10.2 36.5 all-gather.5
  49.1 34.4 all-gather.9
  87.4 77.0 reduce-scatter.14
  168.7 77.9 reduce-scatter.10
  251.0 78.0 reduce-scatter.6
  331.2 61.2 all-gather.13
  395.4 60.4 all-gather.7
  458.8 60.4 all-gather.11
  521.7 65.5 reduce-scatter.16
  589.6 63.9 reduce-scatter.8
  656.0 63.9 reduce-scatter.12
where the time goes:
time: 729 us; the launch traced here: 728 us
  waiting for transfers between devices  647 us (89%)
  matrix products  58.7 us (8%)
  between operations  14 us (2%)
    reduce_scatter x3, waiting for transfers between devices, edata_sum(): lax.psum_scatter(term_fn(jnp.int32(0), share_rows * lax.axis_size('edata'...  230 us
    reduce_scatter x3, waiting for transfers between devices, tensor_sum(): lax.psum_scatter(term_fn(jnp.int32(0), owner_rows * lax.axis_size('tensor...  180 us
    all_gather x3, waiting for transfers between devices, edata_sum(): acted = lax.all_gather(act_fn(summed), 'edata', axis=0, tiled=True)  173 us
    all_gather x1, waiting for transfers between devices, shards(): lax.all_gather(picked, 'tensor', axis=0, tiled=True)  34.4 us
    all_gather x1, waiting for transfers between devices, shards(): lax.all_gather(scaled, 'tensor', axis=0, tiled=True)  28.7 us
  transfers between devices with their start and end apart: 11, of which 11 were waited for; matrix products, arithmetic and copies ran while one was open for 8% of the time, Pallas kernels for 0%

commit v1 on v0

--- a/solution.py
+++ b/solution.py
@@ -5,6 +5,11 @@
 
 EXP_WIN = 2
 CAP = 48
+
+
+def shape_the_sectors(patch):
+    y1 = jnp.stack(lax.psum(1, "tensor") * [patch], 0)
+    return jnp.concatenate(lax.all_to_all(y1, "tensor", 0, 0), 0)
 
 
 def tables(expert_ids, route_weight):
@@ -43,7 +48,7 @@
         "cet,td->ced", combine, cotangent.astype(jnp.float32), precision=lax.Precision.HIGHEST
     ).astype(jnp.bfloat16)
     gathered_x, gathered_g = (
-        lax.all_gather(picked, "tensor", axis=0, tiled=True),
+        shape_the_sectors(picked),
         lax.all_gather(scaled, "tensor", axis=0, tiled=True),
     )
     routed = gathered_x.shape[0]

time: 729 us -> 681 us (0.934)
  waiting for transfers between devices: 647 us -> 544 us
  blocking collectives: 0 us -> 44.8 us
  local copies, waits for them, and re-layouts: 2.07 us -> 10.9 us
    reduce_scatter x3 -> x2, waiting for transfers between devices: 180 us -> 129 us  [tensor_sum(): lax.psum_scatter(term_fn(jnp.int32(0), owner_rows * lax.axis_size('tensor...]
    all_to_all x0 -> x1, blocking collectives: none -> 44.8 us  [shape_the_sectors(): return jnp.concatenate(lax.all_to_all(y1, 'tensor', 0, 0), 0)]
    all_gather x1 -> x0, waiting for transfers between devices: 34.4 us -> none  [shards(): lax.all_gather(picked, 'tensor', axis=0, tiled=True)]
    all_gather x1, waiting for transfers between devices: 28.7 us -> 0.02 us  [shards(): lax.all_gather(scaled, 'tensor', axis=0, tiled=True)]
    unnamed x11, waiting for transfers between devices: 0.86 us -> 25.2 us
    all_gather x3, waiting for transfers between devices: 173 us -> 164 us  [edata_sum(): acted = lax.all_gather(act_fn(summed), 'edata', axis=0, tiled=True)]
  transfers between devices with their start and end apart: 11 -> 10, of which waited for: 11 -> 9; matrix products, arithmetic and copies ran while one was open for 8% -> 10% of each run, Pallas kernels for 0% -> 0%
where the time goes in v1:
time: 681 us
  waiting for transfers between devices  544 us (80%)
  matrix products  57.5 us (8%)
  blocking collectives  44.8 us (7%)
  between operations  16.1 us (2%)
  local copies, waits for them, and re-layouts  10.9 us (2%)
    reduce_scatter x3, waiting for transfers between devices, edata_sum(): lax.psum_scatter(term_fn(jnp.int32(0), share_rows * lax.axis_size('edata'...  226 us
    all_gather x3, waiting for transfers between devices, edata_sum(): acted = lax.all_gather(act_fn(summed), 'edata', axis=0, tiled=True)  164 us
    reduce_scatter x2, waiting for transfers between devices, tensor_sum(): lax.psum_scatter(term_fn(jnp.int32(0), owner_rows * lax.axis_size('tensor...  129 us
    all_to_all x1, blocking collectives, shape_the_sectors(): return jnp.concatenate(lax.all_to_all(y1, 'tensor', 0, 0), 0)  44.8 us
    unnamed x11, waiting for transfers between devices  25.2 us
    dot_general x2, matrix products, partial_down(): jnp.einsum('ref,efd->red', source, weight, preferred_element_type=jnp.flo...  15.5 us
  transfers between devices with their start and end apart: 10, of which 9 were waited for; matrix products, arithmetic and copies ran while one was open for 10% of the time, Pallas kernels for 0%

profile of v1, /device:TPU:4, one launch (start us, length us, event | category | flops | bytes accessed | tf_op | source)
XLA Modules:
  0.0 680.6 jit_solution(2000074693101633587)
XLA Ops:
  8.1 0.7 fusion.28
  8.8 0.7 select_reduce_fusion.1
  10.3 0.9 convolution_convert_fusion.2
  11.4 1.1 convolution_convert_fusion.3
  12.8 44.8 %all_to_all.5 = bf16[16,48,2,768]{3,1,2,0:T(8,128)(2,1)S(1)} all-to-all(bf16[16,48,2,768]{3,1,2,0:T(8,128)(2,1)S(1)} %stack.8), channel_id=1, replica_groups=mesh['edata'=8,'tensor'=16] {'tensor'}, dimensions={0} | all-to-all | bytes 4718592 | tf_op jit(solution)/shard_map/all_to_all | solution.py:12
  57.8 1.8 copy-done.1
  59.5 4.1 convert_bitcast_fusion
  63.7 5.8 convert_bitcast_fusion.2
  69.7 6.9 %convert_bitcast_fusion.1 = bf16[768,2,1024]{2,0,1:T(8,128)(2,1)} fusion(bf16[768,2,768]{2,0,1:T(8,128)(2,1)} %all-gather.7.cloned.1.call-done, bf16[2,1024,768]{2,1,0:T(8,128)(2,1)} %param.12), kind=kOutput, calls=%fused_computation.9 | convolution fusion | flops 2417491968 | bytes 8650752 | tf_op jit(solution)/shard_map/red,efd->ref/dot_general | solution.py:91
  76.7 63.3 %reduce-scatter.14.cloned.1.call-done = bf16[96,2,1024]{2,0,1:T(8,128)(2,1)} async-done(((bf16[768,2,1024]{2,0,1:T(8,128)(2,1)}), bf16[96,2,1024]{2,0,1:T(8,128)(2,1)}) %reduce-scatter.14.cloned.1.call-update) | async-done | bytes 393232 | tf_op jit(solution)/shard_map/reduce_scatter | solution.py:59
  140.0 2.0 fusion.12
  142.0 80.3 %reduce-scatter.6.cloned.1.call-done = bf16[96,2,1024]{2,0,1:T(8,128)(2,1)} async-done(((bf16[768,2,1024]{2,0,1:T(8,128)(2,1)}), bf16[96,2,1024]{2,0,1:T(8,128)(2,1)}) %reduce-scatter.6.cloned.1.call-update) | async-done | bytes 393232 | tf_op jit(solution)/shard_map/reduce_scatter | solution.py:59
  222.4 82.4 %reduce-scatter.10.cloned.1.call-done = bf16[96,2,1024]{2,0,1:T(8,128)(2,1)} async-done(((bf16[768,2,1024]{2,0,1:T(8,128)(2,1)}), bf16[96,2,1024]{2,0,1:T(8,128)(2,1)}) %reduce-scatter.10.cloned.1.call-update) | async-done | bytes 393232 | tf_op jit(solution)/shard_map/reduce_scatter | solution.py:59
  304.8 2.4 fusion.19
  307.2 0.7 all-gather.9.cloned.1.call-update
  308.0 60.1 %all-gather.11.cloned.1.call-done = bf16[768,2,1024]{2,0,1:T(8,128)(2,1)} async-done(((bf16[96,2,1024]{2,0,1:T(8,128)(2,1)}), bf16[768,2,1024]{2,0,1:T(8,128)(2,1)}) %all-gather.11.cloned.1.call-update) | async-done | bytes 3145744 | tf_op jit(solution)/shard_map/all_gather | solution.py:65
  368.1 8.7 %convert_bitcast_fusion.3 = bf16[768,2,768]{0,2,1:T(8,128)(2,1)} fusion(bf16[768,2,1024]{2,0,1:T(8,128)(2,1)} %all-gather.11.cloned.1.call-done, bf16[2,1024,768]{2,1,0:T(8,128)(2,1)} %param.12, bf16[2,1024,768]{2,1,0:T(8,128)(2,1)} %param.14), kind=kOutput, calls=%fused_computation.11 | convolution fusion | flops 2426535936 | bytes 11796480 | tf_op jit(solution)/shard_map/ref,efd->red/dot_general | solution.py:86
  376.7 6.9 %copy.38 = bf16[768,2,768]{2,1,0:T(2,128)(2,1)} copy(bf16[768,2,768]{0,2,1:T(8,128)(2,1)} %convert_bitcast_fusion.3) | data formatting | bytes 4718592 | tf_op jit(solution)/shard_map/convert_element_type | solution.py:70
  383.9 46.7 %all-gather.5.cloned.1.call-done = bf16[768,2,1024]{2,0,1:T(8,128)(2,1)} async-done(((bf16[96,2,1024]{2,0,1:T(8,128)(2,1)}), bf16[768,2,1024]{2,0,1:T(8,128)(2,1)}) %all-gather.5.cloned.1.call-update) | async-done | bytes 3145744 | tf_op jit(solution)/shard_map/all_gather | solution.py:65
  430.6 6.8 %convert_bitcast_fusion.5 = bf16[768,2,768]{2,0,1:T(8,128)(2,1)} fusion(bf16[768,2,1024]{2,0,1:T(8,128)(2,1)} %all-gather.5.cloned.1.call-done, bf16[2,1024,768]{2,1,0:T(8,128)(2,1)} %param.12), kind=kOutput, calls=%fused_computation.13 | convolution fusion | flops 2417098752 | bytes 8650752 | tf_op jit(solution)/shard_map/ref,efd->red/dot_general | solution.py:86
  437.6 56.8 %all-gather.9.cloned.1.call-done = bf16[768,2,1024]{2,0,1:T(8,128)(2,1)} async-done(((bf16[96,2,1024]{2,0,1:T(8,128)(2,1)}), bf16[768,2,1024]{2,0,1:T(8,128)(2,1)}) %all-gather.9.cloned.1.call-update) | async-done | bytes 3145744 | tf_op jit(solution)/shard_map/all_gather | solution.py:65
  494.4 6.9 %convert_bitcast_fusion.4 = bf16[768,2,768]{2,0,1:T(8,128)(2,1)} fusion(bf16[768,2,1024]{2,0,1:T(8,128)(2,1)} %all-gather.9.cloned.1.call-done, bf16[2,768,1024]{2,1,0:T(8,128)(2,1)} %param.11), kind=kOutput, calls=%fused_computation.12 | convolution fusion | flops 2417098752 | bytes 8650752 | tf_op jit(solution)/shard_map/ref,edf->red/dot_general | solution.py:118
  501.3 0.6 dynamic-slice
  502.6 7.1 %convolution_convert_fusion = bf16[2,1024,768]{2,1,0:T(8,128)(2,1)} fusion(bf16[768,2,1024]{2,0,1:T(8,128)(2,1)} %all-gather.5.cloned.1.call-done, bf16[768,2,768]{2,0,1:T(8,128)(2,1)} %all-gather.7.cloned.1.call-done), kind=kOutput, calls=%fused_computation.14 | convolution fusion | flops 2417491968 | bytes 8650752 | tf_op jit(solution)/shard_map/ref,red->efd/dot_general | solution.py:104
  509.7 4.1 convolution_convert_fusion.1
  513.7 24.4 %all-reduce.3.cloned.1.call-done = bf16[768,2,768]{2,1,0:T(2,128)(2,1)} async-done(((bf16[768,2,768]{2,1,0:T(2,128)(2,1)}), bf16[768,2,768]{2,1,0:T(2,128)(2,1)}) %all-reduce.3.cloned.1.call-update) | async-done | bytes 2359312
  538.2 1.0 constant_dynamic-slice_fusion
  539.2 1.0 fusion.8
  540.2 65.0 %reduce-scatter.8.cloned.1.call-done = bf16[48,2,768]{2,0,1:T(8,128)(2,1)} async-done(((bf16[768,2,768]{2,0,1:T(8,128)(2,1)}), bf16[48,2,768]{2,0,1:T(8,128)(2,1)}) %reduce-scatter.8.cloned.1.call-update) | async-done | bytes 147472 | tf_op jit(solution)/shard_map/reduce_scatter | solution.py:69
  605.2 2.0 fusion.6
  607.2 64.3 %reduce-scatter.12.cloned.1.call-done = bf16[48,2,768]{2,0,1:T(8,128)(2,1)} async-done(((bf16[768,2,768]{2,0,1:T(8,128)(2,1)}), bf16[48,2,768]{2,0,1:T(8,128)(2,1)}) %reduce-scatter.12.cloned.1.call-update) | async-done | bytes 147472 | tf_op jit(solution)/shard_map/reduce_scatter | solution.py:69
  671.5 2.0 fusion.7
  (41 shorter events, 2.0 us)
Async XLA Ops:
  8.0 2.3 copy-start
  8.0 61.7 %all-gather.7.cloned.1.call-start = ((), (), s32[]{:S(2)}) async-start(), calls=%async_computation.9 | async-start | bytes 2506752 | tf_op jit(solution)/shard_map/all_gather | solution.py:52
  11.3 128.7 %reduce-scatter.14.cloned.1.call-start = ((), (), s32[]{:S(2)}) async-start(), calls=%async_computation.13 | async-start | bytes 3538944 | tf_op jit(solution)/shard_map/reduce_scatter | solution.py:59
  12.7 45.0 %copy-start.2 = (bf16[2,768,1024]{2,1,0:T(8,128)(2,1)S(1)}, bf16[2,768,1024]{2,1,0:T(8,128)(2,1)}, u32[]{:S(2)}) copy-start(bf16[2,768,1024]{2,1,0:T(8,128)(2,1)} %param.11) | copy-start | bytes 9437188
  57.6 1.9 copy-start.1
  63.7 158.7 %reduce-scatter.6.cloned.1.call-start = ((), (), s32[]{:S(2)}) async-start(), calls=%async_computation.6 | async-start | bytes 3538944 | tf_op jit(solution)/shard_map/reduce_scatter | solution.py:59
  69.6 235.2 %reduce-scatter.10.cloned.1.call-start = ((), (), s32[]{:S(2)}) async-start(), calls=%async_computation.10 | async-start | bytes 3538944 | tf_op jit(solution)/shard_map/reduce_scatter | solution.py:59
  76.6 291.4 %all-gather.11.cloned.1.call-start = ((), (), s32[]{:S(2)}) async-start(), calls=%async_computation.14 | async-start | bytes 3538944 | tf_op jit(solution)/shard_map/all_gather | solution.py:65
  142.0 288.7 %all-gather.5.cloned.1.call-start = ((), (), s32[]{:S(2)}) async-start(), calls=%async_computation.7 | async-start | bytes 3538944 | tf_op jit(solution)/shard_map/all_gather | solution.py:65
  307.2 187.2 %all-gather.9.cloned.1.call-start = ((), (), s32[]{:S(2)}) async-start(), calls=%async_computation.11 | async-start | bytes 3538944 | tf_op jit(solution)/shard_map/all_gather | solution.py:65
  307.9 230.2 %all-reduce.3.cloned.1.call-start = ((), (), s32[]{:S(2)}) async-start(), calls=%async_computation.15 | async-start | bytes 4718592
  383.7 221.5 %reduce-scatter.8.cloned.1.call-start = ((), (), s32[]{:S(2)}) async-start(), calls=%async_computation.8 | async-start | bytes 2506752 | tf_op jit(solution)/shard_map/reduce_scatter | solution.py:69
  437.5 63.8 %copy-start.4 = (u32[128]{0:T(128)S(1)}, u32[128]{0:T(128)}, u32[]{:S(2)}) copy-start(u32[128]{0:T(128)} %constant.29) | copy-start | bytes 1540
  437.5 234.0 %reduce-scatter.12.cloned.1.call-start = ((), (), s32[]{:S(2)}) async-start(), calls=%async_computation.12 | async-start | bytes 2506752 | tf_op jit(solution)/shard_map/reduce_scatter | solution.py:69
  502.5 7.1 %copy-start.3 = (bf16[768,2,1024]{2,0,1:T(8,128)(2,1)S(1)}, bf16[768,2,1024]{2,0,1:T(8,128)(2,1)}, u32[]{:S(2)}) copy-start(bf16[768,2,1024]{2,0,1:T(8,128)(2,1)} %all-gather.9.cloned.1.call-done) | copy-start | bytes 9437188
Sparse Core Ops, SparseCore 0:
  11.4 52.9 all-gather.6
  383.8 154.2 all-reduce.2
  540.6 64.6 reduce-scatter.7
  607.5 63.9 reduce-scatter.11
Sparse Core Ops, SparseCore 1:
  63.8 76.2 reduce-scatter.13
  144.3 78.1 reduce-scatter.5
  226.7 78.1 reduce-scatter.9
  307.2 60.8 all-gather.10
  370.4 60.2 all-gather.4
  433.6 60.8 all-gather.8
